TPU v7x, 512 devices: a whole 4x4x16 slice. The times are simulated.
512 devices in a mesh: dx: 8 (over x, core), dy: 2 (over y_hi), band: 32 (over y_lo, z).
Axes of the slice: x: 4, y: 4 (y_hi: 2, y_lo: 2; y = y_hi * 2 + y_lo), z: 16, core: 2. Of those that a mesh axis runs over, the one named last changes fastest.
Arguments:
- orbitals: bfloat16 [128, 96, 8192], P('dx', 'dy', 'band'), may hold values from -6 to 6
- rotation: bfloat16 [2048, 2048], P('band'), may hold values from -0.125 to 0.125
- potential: float32 [4, 128, 96], P(None, 'dx', 'dy'), may hold values from -3 to 1
Outputs:
- rotated: bfloat16 [128, 96, 8192], P('dx', 'dy', 'band')
- applied: bfloat16 [128, 96, 8192], P('dx', 'dy', 'band')
All inputs are finite; a program needn't handle non-finite values.
Results may differ from a plain program's by a relative error of at most 0.0049.
Values may be sent and summed in bfloat16 or wider, within the bound.
No kernel may reach another device: no remote copies, remote signals or barrier semaphores. Data moves between devices by JAX's collectives and lax.ppermute only.
A program may use at most 64 MiB of HBM per device.

v0:
```python
import functools

import jax
import jax.numpy as jnp
from jax import lax
from jax.experimental import pallas as pl
from jax.experimental.pallas import tpu as pltpu
from jax.sharding import PartitionSpec as P


stencil_weights = (-205.0 / 72.0, 8.0 / 5.0, -1.0 / 5.0, 8.0 / 315.0, -1.0 / 560.0)
PLANES = 4
VMEM = pl.BlockSpec(memory_space=pltpu.VMEM)
ANY = pl.BlockSpec(memory_space=pl.ANY)


def half_of_band():
    return lax.axis_size("band") // 2


def spread_kernel(own_ref, other_ref, out_ref, sort_ref):
    wide, double = out_ref.shape[2:]
    columns = wide // PLANES
    ring = half_of_band()
    mine = lax.axis_index("band") // ring
    row = lax.broadcasted_iota(jnp.int32, (2 * wide, 2 * columns), 0) >> 2
    column = lax.broadcasted_iota(jnp.int32, (2 * wide, 2 * columns), 1)
    pick = (row == column).astype(jnp.bfloat16)
    for pair in range(ring):
        lanes = slice(2 * columns * pair, 2 * columns * (pair + 1))
        rows = jnp.concatenate([own_ref[:, lanes], other_ref[:, lanes]], axis=0)
        tall = lax.dot_general(
            pick, rows, (((1,), (1,)), ((), ())), preferred_element_type=jnp.float32
        ).astype(jnp.bfloat16)
        for k in range(2):
            block = 2 * pair + k
            side = jnp.where(mine == block // ring, 0, 1)
            out_ref[side, block % ring] = tall[k * wide : (k + 1) * wide]
    total = PLANES * double
    i = lax.broadcasted_iota(jnp.int32, (total, total), 0)
    j = lax.broadcasted_iota(jnp.int32, (total, total), 1)
    shift = double.bit_length() - 1
    sort_ref[...] = (((i & (double - 1)) << 2) + (i >> shift) == j).astype(jnp.bfloat16)


def spread(own, other):
    bands, total = own.shape
    wide = bands * PLANES
    return pl.pallas_call(
        spread_kernel,
        in_specs=[VMEM] * 2,
        out_specs=[VMEM] * 2,
        out_shape=[
            jax.ShapeDtypeStruct((2, total // bands // 2, wide, 2 * bands), jnp.bfloat16),
            jax.ShapeDtypeStruct((2 * wide, 2 * wide), jnp.bfloat16),
        ],
        cost_estimate=pl.CostEstimate(flops=5 * 10**8, bytes_accessed=3 * 2**20, transcendentals=0),
        name="spread",
    )(own, other)


def rotate_kernel(
    tall_hbm, psi_hbm, sort_ref,
    keep_ref, send_ref, keep_x_ref, send_x_ref, keep_y_ref, send_y_ref,
    tall_ref, psi_ref, total_ref, tall_sem, psi_sem,
):
    count = psi_ref.shape[0]
    copies = []
    for k in range(count):
        copies.append(
            (
                pltpu.make_async_copy(tall_hbm.at[:, k], tall_ref.at[:, k], tall_sem.at[k]),
                pltpu.make_async_copy(psi_hbm.at[k], psi_ref.at[k], psi_sem.at[k]),
            )
        )
        for copy in copies[-1]:
            copy.start()
    lanes, bands = tall_ref.shape[2:]
    plane = lax.broadcasted_iota(jnp.int32, (lanes, bands), 0) & (PLANES - 1)
    masks = [(plane == q).astype(jnp.bfloat16) for q in range(PLANES)]
    for start in range(0, count, 4):
        group = range(start, min(count, start + 4))
        left, right = [], []
        for k in group:
            for copy in copies[k]:
                copy.wait()
            for side in range(2):
                left.append(psi_ref[k, side])
                tall = tall_ref[side, k]
                right.append(jnp.concatenate([tall * mask for mask in masks], axis=1))
        part = jnp.dot(
            jnp.concatenate(left, axis=1),
            jnp.concatenate(right, axis=0),
            preferred_element_type=jnp.float32,
        )
        if start:
            total_ref[...] += part
        else:
            total_ref[...] = part
    both = jnp.dot(
        total_ref[...].astype(jnp.bfloat16), sort_ref[...], preferred_element_type=jnp.float32
    ).astype(jnp.bfloat16)
    near, far = both[:, :lanes], both[:, lanes:]
    keep_ref[...] = near
    send_ref[...] = far
    tall = keep_x_ref.shape[0]
    mine = lax.axis_index("band") // half_of_band()
    edge = pl.multiple_of(mine * tall, tall)
    keep_x_ref[...] = keep_ref[pl.ds(edge, tall)]
    send_x_ref[...] = send_ref[pl.ds(edge, tall)]
    cells_x = keep_y_ref.shape[0]
    near = near.reshape(cells_x, -1, lanes)
    far = far.reshape(cells_x, -1, lanes)
    cells_y = near.shape[1]
    second = lax.axis_index("dy")

    @pl.when(second == 0)
    def _():
        keep_y_ref[...] = near[:, cells_y - 4 :]
        send_y_ref[...] = far[:, cells_y - 4 :]

    @pl.when(second != 0)
    def _():
        keep_y_ref[...] = near[:, :4]
        send_y_ref[...] = far[:, :4]


def rotate(tall, psi, sort, cells):
    count, _, points, lanes = psi.shape
    total = (points, PLANES * tall.shape[3])
    cells_x, cells_y = cells
    half = jax.ShapeDtypeStruct((points, lanes), jnp.bfloat16)
    x_edge = jax.ShapeDtypeStruct((4 * cells_y, lanes), jnp.bfloat16)
    y_edge = jax.ShapeDtypeStruct((cells_x, 4, lanes), jnp.bfloat16)
    return pl.pallas_call(
        rotate_kernel,
        in_specs=[ANY, ANY, VMEM],
        out_specs=[VMEM] * 6,
        out_shape=[half, half, x_edge, x_edge, y_edge, y_edge],
        scratch_shapes=[
            pltpu.VMEM(tall.shape, jnp.bfloat16),
            pltpu.VMEM(psi.shape, jnp.bfloat16),
            pltpu.VMEM(total, jnp.float32),
            pltpu.SemaphoreType.DMA((count,)),
            pltpu.SemaphoreType.DMA((count,)),
        ],
        name="rotate",
    )(tall, psi, sort)


def stencil_kernel(
    keep_ref, got_ref, keep_x_ref, send_x_ref, keep_y_ref, send_y_ref, levels_ref,
    rotated_ref, out_ref, pad_ref,
):
    cells_x, cells_y, lanes = rotated_ref.shape
    half = cells_x // 2
    rows = slice(8, 8 + cells_y)
    mine = lax.axis_index("band") // half_of_band()
    near, far = half * mine, half * (1 - mine)
    rotated_ref[pl.ds(near, half)] = keep_ref[...]
    rotated_ref[pl.ds(far, half)] = got_ref[...]
    pad_ref[pl.ds(4 + near, half), rows] = keep_ref[...].astype(jnp.float32)
    pad_ref[pl.ds(4 + far, half), rows] = got_ref[...].astype(jnp.float32)
    reach = cells_x + 4
    pad_ref[pl.ds(reach * (1 - mine), 4), rows] = keep_x_ref[...].astype(jnp.float32)
    pad_ref[pl.ds(reach * mine, 4), rows] = send_x_ref[...].astype(jnp.float32)
    keep_y = keep_y_ref[...].astype(jnp.float32)
    send_y = send_y_ref[...].astype(jnp.float32)
    first = lax.axis_index("dy") == 0
    above = slice(8 + cells_y, 12 + cells_y)
    pad_ref[pl.ds(4 + near, half), 4:8] = jnp.where(first, 0.0, keep_y)
    pad_ref[pl.ds(4 + far, half), 4:8] = jnp.where(first, 0.0, send_y)
    pad_ref[pl.ds(4 + near, half), above] = jnp.where(first, keep_y, 0.0)
    pad_ref[pl.ds(4 + far, half), above] = jnp.where(first, send_y, 0.0)
    i = lax.broadcasted_iota(jnp.int32, (lanes, lanes), 0)
    j = lax.broadcasted_iota(jnp.int32, (lanes, lanes), 1)
    apart = jnp.abs(i - j)
    weights = jnp.where(apart == 0, 3.0 * stencil_weights[0], 0.0)
    for d in range(1, PLANES):
        weights = jnp.where(apart == d, stencil_weights[d], weights)
    weights = jnp.where(i // PLANES == j // PLANES, weights, 0.0)
    terms = []
    for _ in range(3):
        terms.append(weights.astype(jnp.bfloat16))
        weights = weights - terms[-1].astype(jnp.float32)
    q = lax.broadcasted_iota(jnp.int32, (PLANES, lanes), 1) & (PLANES - 1)
    cover = (q == lax.broadcasted_iota(jnp.int32, (PLANES, lanes), 0)).astype(jnp.float32)
    for x in range(cells_x):
        laplace = jnp.dot(rotated_ref[x], terms[2], preferred_element_type=jnp.float32)
        laplace += jnp.dot(rotated_ref[x], terms[1], preferred_element_type=jnp.float32)
        laplace += jnp.dot(rotated_ref[x], terms[0], preferred_element_type=jnp.float32)
        for d in range(1, 5):
            total = pad_ref[x + 4 + d, rows] + pad_ref[x + 4 - d, rows]
            total += pad_ref[x + 4, 8 + d : 8 + d + cells_y] + pad_ref[x + 4, 8 - d : 8 - d + cells_y]
            laplace += stencil_weights[d] * total
        field = lax.dot_general(
            levels_ref[:, x],
            cover,
            (((0,), (0,)), ((), ())),
            precision=lax.Precision.HIGHEST,
            preferred_element_type=jnp.float32,
        )
        out_ref[x] = (field * pad_ref[x + 4, rows] - 0.5 * laplace).astype(jnp.bfloat16)


def stencil(*arrays):
    half, cells_y, lanes = arrays[0].shape
    cells_x = 2 * half
    out = jax.ShapeDtypeStruct((cells_x, cells_y, lanes), jnp.bfloat16)
    return pl.pallas_call(
        stencil_kernel,
        in_specs=[VMEM] * len(arrays),
        out_specs=[VMEM] * 2,
        out_shape=[out, out],
        scratch_shapes=[pltpu.VMEM((cells_x + 8, cells_y + 16, lanes), jnp.float32)],
        name="stencil",
    )(*arrays)


def on_device(orbitals, rotation, potential):
    cells_x, cells_y, lanes = orbitals.shape
    half = cells_x // 2
    points = half * cells_y
    columns = lax.axis_size("band")
    ring = columns // 2
    mine = lax.axis_index("band") // ring
    across = [(i, (i + ring) % columns) for i in range(columns)]

    sent = lax.dynamic_slice_in_dim(orbitals, half * (1 - mine), half, 0)
    kept = lax.dynamic_slice_in_dim(orbitals, half * mine, half, 0)
    came = lax.ppermute(sent, "band", across)
    both = jnp.stack([kept, came]).reshape(1, 2, points, lanes)
    groups = [list(range(ring)), list(range(ring, columns))]
    psi = lax.all_gather(both, "band", axis=0, tiled=True, axis_index_groups=groups)
    tall, sort = spread(rotation, lax.ppermute(rotation, "band", across))
    out = rotate(tall, psi, sort, (half, cells_y))
    keep, send, keep_x, send_x, keep_y, send_y = out

    ends = lax.axis_size("dx") - 1
    near, cross = [], []
    for x in range(ends):
        for i in range(ring):
            low, high = i, ring + i
            near += [(x * columns + high, (x + 1) * columns + high)]
            near += [((x + 1) * columns + low, x * columns + low)]
            cross += [(x * columns + high, (x + 1) * columns + low)]
            cross += [((x + 1) * columns + low, x * columns + high)]
    got = lax.ppermute(send, "band", across)
    keep_x = lax.ppermute(keep_x, ("dx", "band"), near)
    send_x = lax.ppermute(send_x, ("dx", "band"), cross)
    keep_y = lax.ppermute(keep_y, "dy", [(0, 1), (1, 0)])
    turn = [
        (y * columns + i, (1 - y) * columns + (i + ring) % columns)
        for y in range(2)
        for i in range(columns)
    ]
    send_y = lax.ppermute(send_y, ("dy", "band"), turn)
    shape = (half, cells_y, lanes)
    edge = (4, cells_y, lanes)
    rotated, applied = stencil(
        keep.reshape(shape), got.reshape(shape), keep_x.reshape(edge), send_x.reshape(edge),
        keep_y, send_y, potential,
    )
    return rotated, applied


def solution(mesh):
    return jax.shard_map(
        on_device,
        mesh=mesh,
        in_specs=(P("dx", "dy", "band"), P("band", None), P(None, "dx", "dy")),
        out_specs=(P("dx", "dy", "band"), P("dx", "dy", "band")),
        check_vma=False,
    )
```

profile of v0, /device:TPU:1, one launch (start us, length us, event | category | flops | bytes accessed | tf_op | source)
XLA Modules:
  0.0 147.8 jit_solution(13103802035713475169)
XLA Ops:
  7.2 0.0 all-gather.2.cloned.1.call-start
  7.2 1.1 constant_dynamic-slice_fusion.1
  8.3 4.0 %collective-permute-start.1 = (bf16[8,48,256]{2,1,0:T(8,128)(2,1)S(1)}, bf16[8,48,256]{2,1,0:T(8,128)(2,1)S(1)}, u32[]{:S(2)}, u32[]{:S(2)}) collective-permute-start(bf16[8,48,256]{2,1,0:T(8,128)(2,1)S(1)} %get-tuple-element.19), channel_id=1, source_target_pairs={{0,16},{1,17},{2,18},{3,19},{4,20},{5,21},{6,22},{7,23},{8,24},{9,... | collective-permute-start | bytes 589832 | tf_op jit(solution)/shard_map/ppermute | solution.py:231
  12.3 3.0 %collective-permute-done.1 = bf16[8,48,256]{2,1,0:T(8,128)(2,1)S(1)} collective-permute-done((bf16[8,48,256]{2,1,0:T(8,128)(2,1)S(1)}, bf16[8,48,256]{2,1,0:T(8,128)(2,1)S(1)}, u32[]{:S(2)}, u32[]{:S(2)}) %collective-permute-start.1) | collective-permute-done | bytes 196640 | tf_op jit(solution)/shard_map/ppermute | solution.py:231
  15.4 0.8 pad_maximum_fusion
  16.1 0.0 all-gather.2.cloned.1.call-update
  16.2 3.4 %collective-permute-start = (bf16[64,2048]{1,0:T(8,128)(2,1)}, bf16[64,2048]{1,0:T(8,128)(2,1)S(1)}, u32[]{:S(2)}, u32[]{:S(2)}) collective-permute-start(bf16[64,2048]{1,0:T(8,128)(2,1)} %own_ref.1), channel_id=1, source_target_pairs={{0,16},{1,17},{2,18},{3,19},{4,20},{5,21},{6,22},{7,23},{8,24},{9,... | collective-permute-start | bytes 786440 | tf_op jit(solution)/shard_map/ppermute | solution.py:235
  19.5 5.3 %collective-permute-done.other_ref = bf16[64,2048]{1,0:T(8,128)(2,1)S(1)} collective-permute-done((bf16[64,2048]{1,0:T(8,128)(2,1)}, bf16[64,2048]{1,0:T(8,128)(2,1)S(1)}, u32[]{:S(2)}, u32[]{:S(2)}) %collective-permute-start) | collective-permute-done | bytes 262176 | tf_op jit(solution)/shard_map/ppermute | solution.py:235
  24.8 0.0 copy-start.5
  24.8 0.7 copy-done.5
  25.5 3.2 %spread.1 = (bf16[2,16,256,128]{3,2,1,0:T(8,128)(2,1)}, bf16[512,512]{1,0:T(8,128)(2,1)}) custom-call(bf16[64,2048]{1,0:T(8,128)(2,1)} %own_ref.1, bf16[64,2048]{1,0:T(8,128)(2,1)} %copy-done.5), custom_call_target="tpu_custom_call" | custom-call | flops 500000000 | bytes 3145728 | tf_op jit(solution)/shard_map/spread/pallas_call | solution.py:49
  28.8 77.4 %all-gather.2.cloned.1.call-done.psi_hbm = bf16[16,2,384,256]{3,2,1,0:T(8,128)(2,1)} async-done(((bf16[1,2,384,256]{3,2,1,0:T(8,128)(2,1)}), bf16[16,2,384,256]{3,2,1,0:T(8,128)(2,1)}) %all-gather.2.cloned.1.call-update) | async-done | bytes 6291472 | tf_op jit(solution)/shard_map/all_gather | solution.py:234
  106.1 8.7 %rotate.1 = (bf16[384,256]{1,0:T(8,128)(2,1)}, bf16[384,256]{1,0:T(8,128)(2,1)}, bf16[192,256]{1,0:T(8,128)(2,1)}, bf16[192,256]{1,0:T(8,128)(2,1)}, bf16[8,4,25...) custom-call(bf16[2,16,256,128]{3,2,1,0:T(8,128)(2,1)} %get-tuple-element.10.tall_hbm, ...), custom_call_target="tpu_custom_call" | custom-call | tf_op jit(solution)/shard_map/rotate/pallas_call | solution.py:135
  114.8 3.1 %collective-permute-start.2 = (bf16[384,256]{1,0:T(8,128)(2,1)}, bf16[384,256]{1,0:T(8,128)(2,1)S(1)}, u32[]{:S(2)}, u32[]{:S(2)}) collective-permute-start(bf16[384,256]{1,0:T(8,128)(2,1)} %get-tuple-element.13), channel_id=1, source_target_pairs={{0,16},{1,17},{2,18},{3,19},{4,20},{5,21},{6,22},{7,23},{8,24},{9,... | collective-permute-start | bytes 589832 | tf_op jit(solution)/shard_map/ppermute | solution.py:248
  118.0 6.1 %collective-permute-start.3 = (bf16[192,256]{1,0:T(8,128)(2,1)}, bf16[192,256]{1,0:T(8,128)(2,1)S(1)}, u32[]{:S(2)}, u32[]{:S(2)}) collective-permute-start(bf16[192,256]{1,0:T(8,128)(2,1)} %get-tuple-element.14), channel_id=1, source_target_pairs={{16,80},{64,0},{17,81},{65,1},{18,82},{66,2},{19,83},{67,3},{20,84... | collective-permute-start | bytes 294920 | tf_op jit(solution)/shard_map/ppermute | solution.py:249
  124.1 1.9 %collective-permute-start.4 = (bf16[192,256]{1,0:T(8,128)(2,1)}, bf16[192,256]{1,0:T(8,128)(2,1)S(1)}, u32[]{:S(2)}, u32[]{:S(2)}) collective-permute-start(bf16[192,256]{1,0:T(8,128)(2,1)} %get-tuple-element.15), channel_id=1, source_target_pairs={{16,64},{64,16},{17,65},{65,17},{18,66},{66,18},{19,67},{67,19},{2... | collective-permute-start | bytes 294920 | tf_op jit(solution)/shard_map/ppermute | solution.py:250
  126.0 4.3 %collective-permute-start.5 = (bf16[8,4,256]{2,1,0:T(4,128)(2,1)}, bf16[8,4,256]{2,1,0:T(4,128)(2,1)S(1)}, u32[]{:S(2)}, u32[]{:S(2)}) collective-permute-start(bf16[8,4,256]{2,1,0:T(4,128)(2,1)} %get-tuple-element.16), channel_id=1, source_target_pairs={{0,32},{32,0},{1,33},{33,1},{2,34},{34,2},{3,35},{35,3},{4,36},{36... | collective-permute-start | bytes 49160 | tf_op jit(solution)/shard_map/ppermute | solution.py:251
  130.3 4.1 %collective-permute-start.6 = (bf16[8,4,256]{2,1,0:T(4,128)(2,1)}, bf16[8,4,256]{2,1,0:T(4,128)(2,1)S(1)}, u32[]{:S(2)}, u32[]{:S(2)}) collective-permute-start(bf16[8,4,256]{2,1,0:T(4,128)(2,1)} %get-tuple-element.17), channel_id=1, source_target_pairs={{0,48},{1,49},{2,50},{3,51},{4,52},{5,53},{6,54},{7,55},{8,56},{9,... | collective-permute-start | bytes 49160 | tf_op jit(solution)/shard_map/ppermute | solution.py:257
  134.5 0.0 collective-permute-done.5.keep_y_ref
  134.5 0.0 copy-start.3
  134.5 1.8 %collective-permute-done.6.send_y_ref = bf16[8,4,256]{2,1,0:T(4,128)(2,1)S(1)} collective-permute-done((bf16[8,4,256]{2,1,0:T(4,128)(2,1)}, bf16[8,4,256]{2,1,0:T(4,128)(2,1)S(1)}, u32[]{:S(2)}, u32[]{:S(2)}) %collective-permute-start.6) | collective-permute-done | bytes 16416 | tf_op jit(solution)/shard_map/ppermute | solution.py:257
  136.3 0.0 copy-start.4
  136.3 0.0 collective-permute-done.3
  136.3 0.0 copy-start.1
  136.3 0.0 collective-permute-done.4
  136.3 0.0 copy-start.2
  136.3 0.0 collective-permute-done.2
  136.3 0.0 copy-start
  136.3 0.0 copy-done.3
  136.3 0.5 copy-done.4
  136.8 0.1 copy-done.1
  136.9 0.0 copy-done.2
  136.9 0.1 copy-done
  137.0 4.0 %stencil.1 = (bf16[16,48,256]{2,1,0:T(8,128)(2,1)}, bf16[16,48,256]{2,1,0:T(8,128)(2,1)}) custom-call(bf16[8,48,256]{2,1,0:T(8,128)(2,1)} %bitcast.7, bf16[8,48,256]{2,1,0:T(8,128)(2,1)} %bitcast.8, bf16[4,48,256]{2,1,0:T(8,128)(2,1)} %bitcast.10, bf16[4,48,256]{2,1,0:T(8,128)(2,1)} %bitcast.11, bf16[8,4,256]{2,1,0:T(4,128)(2,1)} %copy-done.3, ...), custom_call_target="tpu_custom_call" | custom-call | tf_op jit(solution)/shard_map/stencil/pallas_call | solution.py:210
Async XLA Ops:
  7.2 99.0 %all-gather.2.cloned.1.call-start = ((), (), s32[]{:S(2)}) async-start(), calls=%async_computation | async-start | bytes 6684672 | tf_op jit(solution)/shard_map/all_gather | solution.py:234
  8.3 7.1 %collective-permute-start.1 = (bf16[8,48,256]{2,1,0:T(8,128)(2,1)S(1)}, bf16[8,48,256]{2,1,0:T(8,128)(2,1)S(1)}, u32[]{:S(2)}, u32[]{:S(2)}) collective-permute-start(bf16[8,48,256]{2,1,0:T(8,128)(2,1)S(1)} %get-tuple-element.19), channel_id=1, source_target_pairs={{0,16},{1,17},{2,18},{3,19},{4,20},{5,21},{6,22},{7,23},{8,24},{9,... | collective-permute-start | bytes 589832 | tf_op jit(solution)/shard_map/ppermute | solution.py:231
  16.2 8.6 %collective-permute-start = (bf16[64,2048]{1,0:T(8,128)(2,1)}, bf16[64,2048]{1,0:T(8,128)(2,1)S(1)}, u32[]{:S(2)}, u32[]{:S(2)}) collective-permute-start(bf16[64,2048]{1,0:T(8,128)(2,1)} %own_ref.1), channel_id=1, source_target_pairs={{0,16},{1,17},{2,18},{3,19},{4,20},{5,21},{6,22},{7,23},{8,24},{9,... | collective-permute-start | bytes 786440 | tf_op jit(solution)/shard_map/ppermute | solution.py:235
  24.8 0.7 copy-start.5
  114.8 21.4 %collective-permute-start.2 = (bf16[384,256]{1,0:T(8,128)(2,1)}, bf16[384,256]{1,0:T(8,128)(2,1)S(1)}, u32[]{:S(2)}, u32[]{:S(2)}) collective-permute-start(bf16[384,256]{1,0:T(8,128)(2,1)} %get-tuple-element.13), channel_id=1, source_target_pairs={{0,16},{1,17},{2,18},{3,19},{4,20},{5,21},{6,22},{7,23},{8,24},{9,... | collective-permute-start | bytes 589832 | tf_op jit(solution)/shard_map/ppermute | solution.py:248
  118.0 18.3 %collective-permute-start.3 = (bf16[192,256]{1,0:T(8,128)(2,1)}, bf16[192,256]{1,0:T(8,128)(2,1)S(1)}, u32[]{:S(2)}, u32[]{:S(2)}) collective-permute-start(bf16[192,256]{1,0:T(8,128)(2,1)} %get-tuple-element.14), channel_id=1, source_target_pairs={{16,80},{64,0},{17,81},{65,1},{18,82},{66,2},{19,83},{67,3},{20,84... | collective-permute-start | bytes 294920 | tf_op jit(solution)/shard_map/ppermute | solution.py:249
  124.1 12.2 %collective-permute-start.4 = (bf16[192,256]{1,0:T(8,128)(2,1)}, bf16[192,256]{1,0:T(8,128)(2,1)S(1)}, u32[]{:S(2)}, u32[]{:S(2)}) collective-permute-start(bf16[192,256]{1,0:T(8,128)(2,1)} %get-tuple-element.15), channel_id=1, source_target_pairs={{16,64},{64,16},{17,65},{65,17},{18,66},{66,18},{19,67},{67,19},{2... | collective-permute-start | bytes 294920 | tf_op jit(solution)/shard_map/ppermute | solution.py:250
  126.0 8.5 %collective-permute-start.5 = (bf16[8,4,256]{2,1,0:T(4,128)(2,1)}, bf16[8,4,256]{2,1,0:T(4,128)(2,1)S(1)}, u32[]{:S(2)}, u32[]{:S(2)}) collective-permute-start(bf16[8,4,256]{2,1,0:T(4,128)(2,1)} %get-tuple-element.16), channel_id=1, source_target_pairs={{0,32},{32,0},{1,33},{33,1},{2,34},{34,2},{3,35},{35,3},{4,36},{36... | collective-permute-start | bytes 49160 | tf_op jit(solution)/shard_map/ppermute | solution.py:251
  130.3 5.9 %collective-permute-start.6 = (bf16[8,4,256]{2,1,0:T(4,128)(2,1)}, bf16[8,4,256]{2,1,0:T(4,128)(2,1)S(1)}, u32[]{:S(2)}, u32[]{:S(2)}) collective-permute-start(bf16[8,4,256]{2,1,0:T(4,128)(2,1)} %get-tuple-element.17), channel_id=1, source_target_pairs={{0,48},{1,49},{2,50},{3,51},{4,52},{5,53},{6,54},{7,55},{8,56},{9,... | collective-permute-start | bytes 49160 | tf_op jit(solution)/shard_map/ppermute | solution.py:257
  134.5 1.8 %copy-start.3 = (bf16[8,4,256]{2,1,0:T(4,128)(2,1)}, bf16[8,4,256]{2,1,0:T(4,128)(2,1)S(1)}, u32[]{:S(2)}) copy-start(bf16[8,4,256]{2,1,0:T(4,128)(2,1)S(1)} %collective-permute-done.5.keep_y_ref) | copy-start | bytes 49156
  136.3 0.6 copy-start.4
  136.3 0.7 copy-start.1
  136.3 0.7 copy-start.2
  136.3 0.7 copy-start
Sparse Core Ops, SparseCore 0:
  16.3 89.7 all-gather.1
where the time goes:
time: 150 us; the launch traced here: 148 us
  waiting for transfers between devices  87.5 us (58%)
  starting transfers between devices  27 us (18%)
  Pallas kernels  15.9 us (11%)
  between operations  14.2 us (9%)
  local copies, waits for them, and re-layouts  2.47 us (2%)
    all_gather x1, waiting for transfers between devices, on_device(): lax.all_gather(both, 'band', axis=0, tiled=True, axis_index_groups=groups)  77.4 us
    pallas_call x1, Pallas kernels, rotate(): pl.pallas_call(rotate_kernel, in_specs=[ANY, ANY, VMEM], out_specs=[VMEM]...  8.71 us
    ppermute x1, starting transfers between devices, on_device(): keep_x = lax.ppermute(keep_x, ('dx', 'band'), near)  6.09 us
    ppermute x1, waiting for transfers between devices, on_device(): tall, sort = spread(rotation, lax.ppermute(rotation, 'band', across))  5.27 us
    ppermute x1, starting transfers between devices, on_device(): keep_y = lax.ppermute(keep_y, 'dy', [(0, 1), (1, 0)])  4.34 us
    ppermute x1, starting transfers between devices, on_device(): send_y = lax.ppermute(send_y, ('dy', 'band'), turn)  4.12 us
    ppermute x1, starting transfers between devices, on_device(): came = lax.ppermute(sent, 'band', across)  4.02 us
    pallas_call x1, Pallas kernels, stencil(): pl.pallas_call(stencil_kernel, in_specs=[VMEM] * len(arrays), out_specs=[...  3.99 us
  transfers between devices with their start and end apart: 8, of which 4 were waited for; matrix products, arithmetic and copies ran while one was open for 0% of the time, Pallas kernels for 2%

commit v1 on v0

--- a/solution.py
+++ b/solution.py
@@ -1,5 +1,3 @@
-import functools
-
 import jax
 import jax.numpy as jnp
 from jax import lax
@@ -18,8 +16,8 @@
     return lax.axis_size("band") // 2
 
 
-def spread_kernel(own_ref, other_ref, out_ref, sort_ref):
-    wide, double = out_ref.shape[2:]
+def spread_kernel(own_ref, other_ref, out_ref):
+    wide = out_ref.shape[2]
     columns = wide // PLANES
     ring = half_of_band()
     mine = lax.axis_index("band") // ring
@@ -36,11 +34,6 @@
             block = 2 * pair + k
             side = jnp.where(mine == block // ring, 0, 1)
             out_ref[side, block % ring] = tall[k * wide : (k + 1) * wide]
-    total = PLANES * double
-    i = lax.broadcasted_iota(jnp.int32, (total, total), 0)
-    j = lax.broadcasted_iota(jnp.int32, (total, total), 1)
-    shift = double.bit_length() - 1
-    sort_ref[...] = (((i & (double - 1)) << 2) + (i >> shift) == j).astype(jnp.bfloat16)
 
 
 def spread(own, other):
@@ -49,20 +42,17 @@
     return pl.pallas_call(
         spread_kernel,
         in_specs=[VMEM] * 2,
-        out_specs=[VMEM] * 2,
-        out_shape=[
-            jax.ShapeDtypeStruct((2, total // bands // 2, wide, 2 * bands), jnp.bfloat16),
-            jax.ShapeDtypeStruct((2 * wide, 2 * wide), jnp.bfloat16),
-        ],
+        out_specs=VMEM,
+        out_shape=jax.ShapeDtypeStruct((2, total // bands // 2, wide, 2 * bands), jnp.bfloat16),
         cost_estimate=pl.CostEstimate(flops=5 * 10**8, bytes_accessed=3 * 2**20, transcendentals=0),
         name="spread",
     )(own, other)
 
 
 def rotate_kernel(
-    tall_hbm, psi_hbm, sort_ref,
+    tall_hbm, psi_hbm,
     keep_ref, send_ref, keep_x_ref, send_x_ref, keep_y_ref, send_y_ref,
-    tall_ref, psi_ref, total_ref, tall_sem, psi_sem,
+    tall_ref, psi_ref, total_ref, sort_ref, tall_sem, psi_sem,
 ):
     count = psi_ref.shape[0]
     copies = []
@@ -76,24 +66,25 @@
         for copy in copies[-1]:
             copy.start()
     lanes, bands = tall_ref.shape[2:]
+    i = lax.broadcasted_iota(jnp.int32, sort_ref.shape, 0)
+    j = lax.broadcasted_iota(jnp.int32, sort_ref.shape, 1)
+    shift = bands.bit_length() - 1
+    sort_ref[...] = (((i & (bands - 1)) << 2) + (i >> shift) == j).astype(jnp.bfloat16)
     plane = lax.broadcasted_iota(jnp.int32, (lanes, bands), 0) & (PLANES - 1)
     masks = [(plane == q).astype(jnp.bfloat16) for q in range(PLANES)]
-    for start in range(0, count, 4):
-        group = range(start, min(count, start + 4))
-        left, right = [], []
-        for k in group:
-            for copy in copies[k]:
-                copy.wait()
-            for side in range(2):
-                left.append(psi_ref[k, side])
-                tall = tall_ref[side, k]
-                right.append(jnp.concatenate([tall * mask for mask in masks], axis=1))
+    for k in range(count):
+        for copy in copies[k]:
+            copy.wait()
+        weights = []
+        for side in range(2):
+            tall = tall_ref[side, k]
+            weights.append(jnp.concatenate([tall * mask for mask in masks], axis=1))
         part = jnp.dot(
-            jnp.concatenate(left, axis=1),
-            jnp.concatenate(right, axis=0),
+            jnp.concatenate([psi_ref[k, 0], psi_ref[k, 1]], axis=1),
+            jnp.concatenate(weights, axis=0),
             preferred_element_type=jnp.float32,
         )
-        if start:
+        if k:
             total_ref[...] += part
         else:
             total_ref[...] = part
@@ -125,7 +116,7 @@
         send_y_ref[...] = far[:, :4]
 
 
-def rotate(tall, psi, sort, cells):
+def rotate(tall, psi, cells):
     count, _, points, lanes = psi.shape
     total = (points, PLANES * tall.shape[3])
     cells_x, cells_y = cells
@@ -134,18 +125,19 @@
     y_edge = jax.ShapeDtypeStruct((cells_x, 4, lanes), jnp.bfloat16)
     return pl.pallas_call(
         rotate_kernel,
-        in_specs=[ANY, ANY, VMEM],
+        in_specs=[ANY, ANY],
         out_specs=[VMEM] * 6,
         out_shape=[half, half, x_edge, x_edge, y_edge, y_edge],
         scratch_shapes=[
             pltpu.VMEM(tall.shape, jnp.bfloat16),
             pltpu.VMEM(psi.shape, jnp.bfloat16),
             pltpu.VMEM(total, jnp.float32),
+            pltpu.VMEM((total[1], total[1]), jnp.bfloat16),
             pltpu.SemaphoreType.DMA((count,)),
             pltpu.SemaphoreType.DMA((count,)),
         ],
         name="rotate",
-    )(tall, psi, sort)
+    )(tall, psi)
 
 
 def stencil_kernel(
@@ -232,8 +224,8 @@
     both = jnp.stack([kept, came]).reshape(1, 2, points, lanes)
     groups = [list(range(ring)), list(range(ring, columns))]
     psi = lax.all_gather(both, "band", axis=0, tiled=True, axis_index_groups=groups)
-    tall, sort = spread(rotation, lax.ppermute(rotation, "band", across))
-    out = rotate(tall, psi, sort, (half, cells_y))
+    tall = spread(rotation, lax.ppermute(rotation, "band", across))
+    out = rotate(tall, psi, (half, cells_y))
     keep, send, keep_x, send_x, keep_y, send_y = out
 
     ends = lax.axis_size("dx") - 1
@@ -245,16 +237,16 @@
             near += [((x + 1) * columns + low, x * columns + low)]
             cross += [(x * columns + high, (x + 1) * columns + low)]
             cross += [((x + 1) * columns + low, x * columns + high)]
-    got = lax.ppermute(send, "band", across)
-    keep_x = lax.ppermute(keep_x, ("dx", "band"), near)
-    send_x = lax.ppermute(send_x, ("dx", "band"), cross)
-    keep_y = lax.ppermute(keep_y, "dy", [(0, 1), (1, 0)])
     turn = [
         (y * columns + i, (1 - y) * columns + (i + ring) % columns)
         for y in range(2)
         for i in range(columns)
     ]
+    keep_y = lax.ppermute(keep_y, "dy", [(0, 1), (1, 0)])
     send_y = lax.ppermute(send_y, ("dy", "band"), turn)
+    got = lax.ppermute(send, "band", across)
+    keep_x = lax.ppermute(keep_x, ("dx", "band"), near)
+    send_x = lax.ppermute(send_x, ("dx", "band"), cross)
     shape = (half, cells_y, lanes)
     edge = (4, cells_y, lanes)
     rotated, applied = stencil(

time: 150 us -> 148 us (0.987)
  Pallas kernels: 15.9 us -> 13.8 us
    pallas_call x2, Pallas kernels: 11.9 us -> 9.83 us  [the longest x1 6.74 us: rotate(): pl.pallas_call(rotate_kernel, in_specs=[ANY, ANY], out_specs=[VMEM] * 6,...]
where the time goes in v1:
time: 148 us; the launch traced here: 146 us
  waiting for transfers between devices  87.6 us (59%)
  starting transfers between devices  27 us (18%)
  between operations  14.2 us (10%)
  Pallas kernels  13.8 us (9%)
  local copies, waits for them, and re-layouts  2.46 us (2%)
    all_gather x1, waiting for transfers between devices, on_device(): lax.all_gather(both, 'band', axis=0, tiled=True, axis_index_groups=groups)  77.5 us
    pallas_call x1, Pallas kernels, rotate(): pl.pallas_call(rotate_kernel, in_specs=[ANY, ANY], out_specs=[VMEM] * 6,...  6.74 us
    ppermute x1, starting transfers between devices, on_device(): keep_x = lax.ppermute(keep_x, ('dx', 'band'), near)  6.09 us
    ppermute x1, waiting for transfers between devices, on_device(): tall = spread(rotation, lax.ppermute(rotation, 'band', across))  5.27 us
    ppermute x1, starting transfers between devices, on_device(): keep_y = lax.ppermute(keep_y, 'dy', [(0, 1), (1, 0)])  4.34 us
    ppermute x1, starting transfers between devices, on_device(): send_y = lax.ppermute(send_y, ('dy', 'band'), turn)  4.12 us
    ppermute x1, starting transfers between devices, on_device(): came = lax.ppermute(sent, 'band', across)  4.02 us
    pallas_call x1, Pallas kernels, stencil(): pl.pallas_call(stencil_kernel, in_specs=[VMEM] * len(arrays), out_specs=[...  3.99 us
  transfers between devices with their start and end apart: 8, of which 4 were waited for; matrix products, arithmetic and copies ran while one was open for 0% of the time, Pallas kernels for 2%

profile of v1, /device:TPU:1, one launch (start us, length us, event | category | flops | bytes accessed | tf_op | source)
XLA Modules:
  0.0 145.9 jit_solution(6364637903498268587)
XLA Ops:
  7.2 0.0 all-gather.2.cloned.1.call-start
  7.2 1.1 constant_dynamic-slice_fusion.1
  8.3 4.0 %collective-permute-start.1 = (bf16[8,48,256]{2,1,0:T(8,128)(2,1)S(1)}, bf16[8,48,256]{2,1,0:T(8,128)(2,1)S(1)}, u32[]{:S(2)}, u32[]{:S(2)}) collective-permute-start(bf16[8,48,256]{2,1,0:T(8,128)(2,1)S(1)} %get-tuple-element.15), channel_id=1, source_target_pairs={{0,16},{1,17},{2,18},{3,19},{4,20},{5,21},{6,22},{7,23},{8,24},{9,... | collective-permute-start | bytes 589832 | tf_op jit(solution)/shard_map/ppermute | solution.py:223
  12.3 3.0 %collective-permute-done.1 = bf16[8,48,256]{2,1,0:T(8,128)(2,1)S(1)} collective-permute-done((bf16[8,48,256]{2,1,0:T(8,128)(2,1)S(1)}, bf16[8,48,256]{2,1,0:T(8,128)(2,1)S(1)}, u32[]{:S(2)}, u32[]{:S(2)}) %collective-permute-start.1) | collective-permute-done | bytes 196640 | tf_op jit(solution)/shard_map/ppermute | solution.py:223
  15.4 0.8 pad_maximum_fusion
  16.1 0.0 all-gather.2.cloned.1.call-update
  16.2 3.4 %collective-permute-start = (bf16[64,2048]{1,0:T(8,128)(2,1)}, bf16[64,2048]{1,0:T(8,128)(2,1)S(1)}, u32[]{:S(2)}, u32[]{:S(2)}) collective-permute-start(bf16[64,2048]{1,0:T(8,128)(2,1)} %own_ref.1), channel_id=1, source_target_pairs={{0,16},{1,17},{2,18},{3,19},{4,20},{5,21},{6,22},{7,23},{8,24},{9,... | collective-permute-start | bytes 786440 | tf_op jit(solution)/shard_map/ppermute | solution.py:227
  19.5 5.3 %collective-permute-done.other_ref = bf16[64,2048]{1,0:T(8,128)(2,1)S(1)} collective-permute-done((bf16[64,2048]{1,0:T(8,128)(2,1)}, bf16[64,2048]{1,0:T(8,128)(2,1)S(1)}, u32[]{:S(2)}, u32[]{:S(2)}) %collective-permute-start) | collective-permute-done | bytes 262176 | tf_op jit(solution)/shard_map/ppermute | solution.py:227
  24.8 0.0 copy-start
  24.8 0.7 copy-done
  25.5 3.1 %spread.1.tall_hbm = bf16[2,16,256,128]{3,2,1,0:T(8,128)(2,1)} custom-call(bf16[64,2048]{1,0:T(8,128)(2,1)} %own_ref.1, bf16[64,2048]{1,0:T(8,128)(2,1)} %copy-done), custom_call_target="tpu_custom_call" | custom-call | flops 500000000 | bytes 3145728 | tf_op jit(solution)/shard_map/spread/pallas_call | solution.py:42
  28.6 77.5 %all-gather.2.cloned.1.call-done.psi_hbm = bf16[16,2,384,256]{3,2,1,0:T(8,128)(2,1)} async-done(((bf16[1,2,384,256]{3,2,1,0:T(8,128)(2,1)}), bf16[16,2,384,256]{3,2,1,0:T(8,128)(2,1)}) %all-gather.2.cloned.1.call-update) | async-done | bytes 6291472 | tf_op jit(solution)/shard_map/all_gather | solution.py:226
  106.1 6.7 %rotate.1 = (bf16[384,256]{1,0:T(8,128)(2,1)}, bf16[384,256]{1,0:T(8,128)(2,1)}, bf16[192,256]{1,0:T(8,128)(2,1)}, bf16[192,256]{1,0:T(8,128)(2,1)}, bf16[8,4,25...) custom-call(bf16[2,16,256,128]{3,2,1,0:T(8,128)(2,1)} %spread.1.tall_hbm, ...), custom_call_target="tpu_custom_call" | custom-call | tf_op jit(solution)/shard_map/rotate/pallas_call | solution.py:126
  112.9 3.1 %collective-permute-start.2 = (bf16[384,256]{1,0:T(8,128)(2,1)}, bf16[384,256]{1,0:T(8,128)(2,1)S(1)}, u32[]{:S(2)}, u32[]{:S(2)}) collective-permute-start(bf16[384,256]{1,0:T(8,128)(2,1)} %get-tuple-element.9), channel_id=1, source_target_pairs={{0,16},{1,17},{2,18},{3,19},{4,20},{5,21},{6,22},{7,23},{8,24},{9,... | collective-permute-start | bytes 589832 | tf_op jit(solution)/shard_map/ppermute | solution.py:247
  116.0 6.1 %collective-permute-start.3 = (bf16[192,256]{1,0:T(8,128)(2,1)}, bf16[192,256]{1,0:T(8,128)(2,1)S(1)}, u32[]{:S(2)}, u32[]{:S(2)}) collective-permute-start(bf16[192,256]{1,0:T(8,128)(2,1)} %get-tuple-element.10), channel_id=1, source_target_pairs={{16,80},{64,0},{17,81},{65,1},{18,82},{66,2},{19,83},{67,3},{20,84... | collective-permute-start | bytes 294920 | tf_op jit(solution)/shard_map/ppermute | solution.py:248
  122.1 1.9 %collective-permute-start.4 = (bf16[192,256]{1,0:T(8,128)(2,1)}, bf16[192,256]{1,0:T(8,128)(2,1)S(1)}, u32[]{:S(2)}, u32[]{:S(2)}) collective-permute-start(bf16[192,256]{1,0:T(8,128)(2,1)} %get-tuple-element.11), channel_id=1, source_target_pairs={{16,64},{64,16},{17,65},{65,17},{18,66},{66,18},{19,67},{67,19},{2... | collective-permute-start | bytes 294920 | tf_op jit(solution)/shard_map/ppermute | solution.py:249
  124.0 4.3 %collective-permute-start.5 = (bf16[8,4,256]{2,1,0:T(4,128)(2,1)}, bf16[8,4,256]{2,1,0:T(4,128)(2,1)S(1)}, u32[]{:S(2)}, u32[]{:S(2)}) collective-permute-start(bf16[8,4,256]{2,1,0:T(4,128)(2,1)} %get-tuple-element.12), channel_id=1, source_target_pairs={{0,32},{32,0},{1,33},{33,1},{2,34},{34,2},{3,35},{35,3},{4,36},{36... | collective-permute-start | bytes 49160 | tf_op jit(solution)/shard_map/ppermute | solution.py:245
  128.4 4.1 %collective-permute-start.6 = (bf16[8,4,256]{2,1,0:T(4,128)(2,1)}, bf16[8,4,256]{2,1,0:T(4,128)(2,1)S(1)}, u32[]{:S(2)}, u32[]{:S(2)}) collective-permute-start(bf16[8,4,256]{2,1,0:T(4,128)(2,1)} %get-tuple-element.13), channel_id=1, source_target_pairs={{0,48},{1,49},{2,50},{3,51},{4,52},{5,53},{6,54},{7,55},{8,56},{9,... | collective-permute-start | bytes 49160 | tf_op jit(solution)/shard_map/ppermute | solution.py:246
  132.5 0.0 collective-permute-done.5.keep_y_ref
  132.5 0.0 copy-start.4
  132.5 1.8 %collective-permute-done.6.send_y_ref = bf16[8,4,256]{2,1,0:T(4,128)(2,1)S(1)} collective-permute-done((bf16[8,4,256]{2,1,0:T(4,128)(2,1)}, bf16[8,4,256]{2,1,0:T(4,128)(2,1)S(1)}, u32[]{:S(2)}, u32[]{:S(2)}) %collective-permute-start.6) | collective-permute-done | bytes 16416 | tf_op jit(solution)/shard_map/ppermute | solution.py:246
  134.3 0.0 copy-start.5
  134.3 0.0 collective-permute-done.3
  134.3 0.0 copy-start.2
  134.3 0.0 collective-permute-done.4
  134.3 0.0 copy-start.3
  134.3 0.0 collective-permute-done.2
  134.3 0.0 copy-start.1
  134.3 0.0 copy-done.4
  134.3 0.6 copy-done.5
  134.9 0.0 copy-done.2
  134.9 0.1 copy-done.3
  135.0 0.1 copy-done.1
  135.0 4.0 %stencil.1 = (bf16[16,48,256]{2,1,0:T(8,128)(2,1)}, bf16[16,48,256]{2,1,0:T(8,128)(2,1)}) custom-call(bf16[8,48,256]{2,1,0:T(8,128)(2,1)} %bitcast.7, bf16[8,48,256]{2,1,0:T(8,128)(2,1)} %bitcast.8, bf16[4,48,256]{2,1,0:T(8,128)(2,1)} %bitcast.10, bf16[4,48,256]{2,1,0:T(8,128)(2,1)} %bitcast.11, bf16[8,4,256]{2,1,0:T(4,128)(2,1)} %copy-done.4, ...), custom_call_target="tpu_custom_call" | custom-call | tf_op jit(solution)/shard_map/stencil/pallas_call | solution.py:202
Async XLA Ops:
  7.2 99.0 %all-gather.2.cloned.1.call-start = ((), (), s32[]{:S(2)}) async-start(), calls=%async_computation | async-start | bytes 6684672 | tf_op jit(solution)/shard_map/all_gather | solution.py:226
  8.3 7.1 %collective-permute-start.1 = (bf16[8,48,256]{2,1,0:T(8,128)(2,1)S(1)}, bf16[8,48,256]{2,1,0:T(8,128)(2,1)S(1)}, u32[]{:S(2)}, u32[]{:S(2)}) collective-permute-start(bf16[8,48,256]{2,1,0:T(8,128)(2,1)S(1)} %get-tuple-element.15), channel_id=1, source_target_pairs={{0,16},{1,17},{2,18},{3,19},{4,20},{5,21},{6,22},{7,23},{8,24},{9,... | collective-permute-start | bytes 589832 | tf_op jit(solution)/shard_map/ppermute | solution.py:223
  16.2 8.6 %collective-permute-start = (bf16[64,2048]{1,0:T(8,128)(2,1)}, bf16[64,2048]{1,0:T(8,128)(2,1)S(1)}, u32[]{:S(2)}, u32[]{:S(2)}) collective-permute-start(bf16[64,2048]{1,0:T(8,128)(2,1)} %own_ref.1), channel_id=1, source_target_pairs={{0,16},{1,17},{2,18},{3,19},{4,20},{5,21},{6,22},{7,23},{8,24},{9,... | collective-permute-start | bytes 786440 | tf_op jit(solution)/shard_map/ppermute | solution.py:227
  24.8 0.7 copy-start
  112.9 21.4 %collective-permute-start.2 = (bf16[384,256]{1,0:T(8,128)(2,1)}, bf16[384,256]{1,0:T(8,128)(2,1)S(1)}, u32[]{:S(2)}, u32[]{:S(2)}) collective-permute-start(bf16[384,256]{1,0:T(8,128)(2,1)} %get-tuple-element.9), channel_id=1, source_target_pairs={{0,16},{1,17},{2,18},{3,19},{4,20},{5,21},{6,22},{7,23},{8,24},{9,... | collective-permute-start | bytes 589832 | tf_op jit(solution)/shard_map/ppermute | solution.py:247
  116.0 18.3 %collective-permute-start.3 = (bf16[192,256]{1,0:T(8,128)(2,1)}, bf16[192,256]{1,0:T(8,128)(2,1)S(1)}, u32[]{:S(2)}, u32[]{:S(2)}) collective-permute-start(bf16[192,256]{1,0:T(8,128)(2,1)} %get-tuple-element.10), channel_id=1, source_target_pairs={{16,80},{64,0},{17,81},{65,1},{18,82},{66,2},{19,83},{67,3},{20,84... | collective-permute-start | bytes 294920 | tf_op jit(solution)/shard_map/ppermute | solution.py:248
  122.1 12.2 %collective-permute-start.4 = (bf16[192,256]{1,0:T(8,128)(2,1)}, bf16[192,256]{1,0:T(8,128)(2,1)S(1)}, u32[]{:S(2)}, u32[]{:S(2)}) collective-permute-start(bf16[192,256]{1,0:T(8,128)(2,1)} %get-tuple-element.11), channel_id=1, source_target_pairs={{16,64},{64,16},{17,65},{65,17},{18,66},{66,18},{19,67},{67,19},{2... | collective-permute-start | bytes 294920 | tf_op jit(solution)/shard_map/ppermute | solution.py:249
  124.0 8.5 %collective-permute-start.5 = (bf16[8,4,256]{2,1,0:T(4,128)(2,1)}, bf16[8,4,256]{2,1,0:T(4,128)(2,1)S(1)}, u32[]{:S(2)}, u32[]{:S(2)}) collective-permute-start(bf16[8,4,256]{2,1,0:T(4,128)(2,1)} %get-tuple-element.12), channel_id=1, source_target_pairs={{0,32},{32,0},{1,33},{33,1},{2,34},{34,2},{3,35},{35,3},{4,36},{36... | collective-permute-start | bytes 49160 | tf_op jit(solution)/shard_map/ppermute | solution.py:245
  128.4 5.9 %collective-permute-start.6 = (bf16[8,4,256]{2,1,0:T(4,128)(2,1)}, bf16[8,4,256]{2,1,0:T(4,128)(2,1)S(1)}, u32[]{:S(2)}, u32[]{:S(2)}) collective-permute-start(bf16[8,4,256]{2,1,0:T(4,128)(2,1)} %get-tuple-element.13), channel_id=1, source_target_pairs={{0,48},{1,49},{2,50},{3,51},{4,52},{5,53},{6,54},{7,55},{8,56},{9,... | collective-permute-start | bytes 49160 | tf_op jit(solution)/shard_map/ppermute | solution.py:246
  132.5 1.8 %copy-start.4 = (bf16[8,4,256]{2,1,0:T(4,128)(2,1)}, bf16[8,4,256]{2,1,0:T(4,128)(2,1)S(1)}, u32[]{:S(2)}) copy-start(bf16[8,4,256]{2,1,0:T(4,128)(2,1)S(1)} %collective-permute-done.5.keep_y_ref) | copy-start | bytes 49156
  134.3 0.6 copy-start.5
  134.3 0.6 copy-start.2
  134.3 0.7 copy-start.3
  134.3 0.7 copy-start.1
Sparse Core Ops, SparseCore 0:
  16.3 89.7 all-gather.1

commit v2 on v1

--- a/solution.py
+++ b/solution.py
@@ -10,6 +10,7 @@
 PLANES = 4
 VMEM = pl.BlockSpec(memory_space=pltpu.VMEM)
 ANY = pl.BlockSpec(memory_space=pl.ANY)
+HBM = pl.BlockSpec(memory_space=pltpu.HBM)
 
 
 def half_of_band():
@@ -45,6 +46,7 @@
         out_specs=VMEM,
         out_shape=jax.ShapeDtypeStruct((2, total // bands // 2, wide, 2 * bands), jnp.bfloat16),
         cost_estimate=pl.CostEstimate(flops=5 * 10**8, bytes_accessed=3 * 2**20, transcendentals=0),
+        compiler_params=pltpu.CompilerParams(vmem_limit_bytes=12 * 2**20),
         name="spread",
     )(own, other)
 
@@ -125,7 +127,7 @@
     y_edge = jax.ShapeDtypeStruct((cells_x, 4, lanes), jnp.bfloat16)
     return pl.pallas_call(
         rotate_kernel,
-        in_specs=[ANY, ANY],
+        in_specs=[ANY, HBM],
         out_specs=[VMEM] * 6,
         out_shape=[half, half, x_edge, x_edge, y_edge, y_edge],
         scratch_shapes=[
@@ -136,14 +138,26 @@
             pltpu.SemaphoreType.DMA((count,)),
             pltpu.SemaphoreType.DMA((count,)),
         ],
+        compiler_params=pltpu.CompilerParams(vmem_limit_bytes=49 * 2**20),
         name="rotate",
     )(tall, psi)
 
 
 def stencil_kernel(
-    keep_ref, got_ref, keep_x_ref, send_x_ref, keep_y_ref, send_y_ref, levels_ref,
-    rotated_ref, out_ref, pad_ref,
+    keep_hbm, got_hbm, keep_x_hbm, send_x_hbm, keep_y_hbm, send_y_hbm, levels_hbm,
+    rotated_ref, out_ref, pad_ref, keep_ref, got_ref, keep_x_ref, send_x_ref, keep_y_ref, send_y_ref, levels_ref,
+    sem,
 ):
+    sources = [keep_hbm, got_hbm, keep_x_hbm, send_x_hbm, keep_y_hbm, send_y_hbm, levels_hbm]
+    targets = [keep_ref, got_ref, keep_x_ref, send_x_ref, keep_y_ref, send_y_ref, levels_ref]
+    copies = [
+        pltpu.make_async_copy(source, target, sem.at[k])
+        for k, (source, target) in enumerate(zip(sources, targets))
+    ]
+    for copy in copies:
+        copy.start()
+    for copy in copies:
+        copy.wait()
     cells_x, cells_y, lanes = rotated_ref.shape
     half = cells_x // 2
     rows = slice(8, 8 + cells_y)
@@ -201,10 +215,15 @@
     out = jax.ShapeDtypeStruct((cells_x, cells_y, lanes), jnp.bfloat16)
     return pl.pallas_call(
         stencil_kernel,
-        in_specs=[VMEM] * len(arrays),
+        in_specs=[ANY] * len(arrays),
         out_specs=[VMEM] * 2,
         out_shape=[out, out],
-        scratch_shapes=[pltpu.VMEM((cells_x + 8, cells_y + 16, lanes), jnp.float32)],
+        scratch_shapes=[
+            pltpu.VMEM((cells_x + 8, cells_y + 16, lanes), jnp.float32),
+            *[pltpu.VMEM(a.shape, a.dtype) for a in arrays],
+            pltpu.SemaphoreType.DMA((len(arrays),)),
+        ],
+        compiler_params=pltpu.CompilerParams(vmem_limit_bytes=12 * 2**20),
         name="stencil",
     )(*arrays)
 

time: 148 us -> 147 us (level)
  Pallas kernels: 13.8 us -> 10.8 us
  waiting for transfers between devices: 87.6 us -> 89.5 us
    pallas_call x1, Pallas kernels: 3.09 us -> 0.71 us  [spread(): pl.pallas_call(spread_kernel, in_specs=[VMEM] * 2, out_specs=VMEM, out_sh...]
    all_gather x1, waiting for transfers between devices: 77.5 us -> 79.6 us  [on_device(): lax.all_gather(both, 'band', axis=0, tiled=True, axis_index_groups=groups)]
  transfers between devices with their start and end apart: 8 -> 8, of which waited for: 4 -> 4; matrix products, arithmetic and copies ran while one was open for 0% -> 0% of each run, Pallas kernels for 2% -> 0%
where the time goes in v2:
time: 147 us; the launch traced here: 144 us
  waiting for transfers between devices  89.5 us (61%)
  starting transfers between devices  27 us (18%)
  between operations  14.2 us (10%)
  Pallas kernels  10.8 us (7%)
  local copies, waits for them, and re-layouts  2.01 us (1%)
    all_gather x1, waiting for transfers between devices, on_device(): lax.all_gather(both, 'band', axis=0, tiled=True, axis_index_groups=groups)  79.6 us
    pallas_call x1, Pallas kernels, rotate(): pl.pallas_call(rotate_kernel, in_specs=[ANY, HBM], out_specs=[VMEM] * 6,...  6.4 us
    ppermute x1, starting transfers between devices, on_device(): keep_x = lax.ppermute(keep_x, ('dx', 'band'), near)  6.09 us
    ppermute x1, waiting for transfers between devices, on_device(): tall = spread(rotation, lax.ppermute(rotation, 'band', across))  5.27 us
    ppermute x1, starting transfers between devices, on_device(): keep_y = lax.ppermute(keep_y, 'dy', [(0, 1), (1, 0)])  4.35 us
    ppermute x1, starting transfers between devices, on_device(): send_y = lax.ppermute(send_y, ('dy', 'band'), turn)  4.12 us
    ppermute x1, starting transfers between devices, on_device(): came = lax.ppermute(sent, 'band', across)  4.02 us
    pallas_call x1, Pallas kernels, stencil(): pl.pallas_call(stencil_kernel, in_specs=[ANY] * len(arrays), out_specs=[V...  3.74 us
  transfers between devices with their start and end apart: 8, of which 4 were waited for; matrix products, arithmetic and copies ran while one was open for 0% of the time, Pallas kernels for 0%

profile of v2, /device:TPU:1, one launch (start us, length us, event | category | flops | bytes accessed | tf_op | source)
XLA Modules:
  0.0 144.4 jit_solution(16231870343090066454)
XLA Ops:
  7.2 0.0 all-gather.2.cloned.1.call-start
  7.2 1.1 constant_dynamic-slice_fusion.1
  8.3 0.0 copy-start.1
  8.3 4.0 %collective-permute-start.1 = (bf16[8,48,256]{2,1,0:T(8,128)(2,1)S(1)}, bf16[8,48,256]{2,1,0:T(8,128)(2,1)S(1)}, u32[]{:S(2)}, u32[]{:S(2)}) collective-permute-start(bf16[8,48,256]{2,1,0:T(8,128)(2,1)S(1)} %get-tuple-element.15), channel_id=1, source_target_pairs={{0,16},{1,17},{2,18},{3,19},{4,20},{5,21},{6,22},{7,23},{8,24},{9,... | collective-permute-start | bytes 589832 | tf_op jit(solution)/shard_map/ppermute | solution.py:242
  12.3 3.0 %collective-permute-done.1 = bf16[8,48,256]{2,1,0:T(8,128)(2,1)S(1)} collective-permute-done((bf16[8,48,256]{2,1,0:T(8,128)(2,1)S(1)}, bf16[8,48,256]{2,1,0:T(8,128)(2,1)S(1)}, u32[]{:S(2)}, u32[]{:S(2)}) %collective-permute-start.1) | collective-permute-done | bytes 196640 | tf_op jit(solution)/shard_map/ppermute | solution.py:242
  15.4 0.8 pad_maximum_fusion
  16.2 0.0 all-gather.2.cloned.1.call-update
  16.2 3.4 %collective-permute-start = (bf16[64,2048]{1,0:T(8,128)(2,1)}, bf16[64,2048]{1,0:T(8,128)(2,1)S(1)}, u32[]{:S(2)}, u32[]{:S(2)}) collective-permute-start(bf16[64,2048]{1,0:T(8,128)(2,1)} %own_ref.1), channel_id=1, source_target_pairs={{0,16},{1,17},{2,18},{3,19},{4,20},{5,21},{6,22},{7,23},{8,24},{9,... | collective-permute-start | bytes 786440 | tf_op jit(solution)/shard_map/ppermute | solution.py:246
  19.6 5.3 %collective-permute-done.other_ref = bf16[64,2048]{1,0:T(8,128)(2,1)S(1)} collective-permute-done((bf16[64,2048]{1,0:T(8,128)(2,1)}, bf16[64,2048]{1,0:T(8,128)(2,1)S(1)}, u32[]{:S(2)}, u32[]{:S(2)}) %collective-permute-start) | collective-permute-done | bytes 262176 | tf_op jit(solution)/shard_map/ppermute | solution.py:246
  24.8 0.0 copy-start
  24.8 0.9 copy-done
  25.8 0.7 spread.1.tall_hbm
  26.5 79.6 %all-gather.2.cloned.1.call-done.psi_hbm = bf16[16,2,384,256]{3,2,1,0:T(8,128)(2,1)} async-done(((bf16[1,2,384,256]{3,2,1,0:T(8,128)(2,1)}), bf16[16,2,384,256]{3,2,1,0:T(8,128)(2,1)}) %all-gather.2.cloned.1.call-update) | async-done | bytes 6291472 | tf_op jit(solution)/shard_map/all_gather | solution.py:245
  106.1 6.4 %rotate.1 = (bf16[384,256]{1,0:T(8,128)(2,1)S(1)}, bf16[384,256]{1,0:T(8,128)(2,1)S(1)}, bf16[192,256]{1,0:T(8,128)(2,1)S(1)}, bf16[192,256]{1,0:T(8,128)(2,1)S(...) custom-call(bf16[2,16,256,128]{3,2,1,0:T(8,128)(2,1)S(1)} %spread.1.tall_hbm, ...), custom_call_target="tpu_custom_call" | custom-call | tf_op jit(solution)/shard_map/rotate/pallas_call | solution.py:128
  112.5 3.1 %collective-permute-start.2 = (bf16[384,256]{1,0:T(8,128)(2,1)S(1)}, bf16[384,256]{1,0:T(8,128)(2,1)S(1)}, u32[]{:S(2)}, u32[]{:S(2)}) collective-permute-start(bf16[384,256]{1,0:T(8,128)(2,1)S(1)} %get-tuple-element.9), channel_id=1, source_target_pairs={{0,16},{1,17},{2,18},{3,19},{4,20},{5,21},{6,22},{7,23},{8,24},{9,... | collective-permute-start | bytes 589832 | tf_op jit(solution)/shard_map/ppermute | solution.py:266
  115.7 6.1 %collective-permute-start.3 = (bf16[192,256]{1,0:T(8,128)(2,1)S(1)}, bf16[192,256]{1,0:T(8,128)(2,1)S(1)}, u32[]{:S(2)}, u32[]{:S(2)}) collective-permute-start(bf16[192,256]{1,0:T(8,128)(2,1)S(1)} %get-tuple-element.10), channel_id=1, source_target_pairs={{16,80},{64,0},{17,81},{65,1},{18,82},{66,2},{19,83},{67,3},{20,84... | collective-permute-start | bytes 294920 | tf_op jit(solution)/shard_map/ppermute | solution.py:267
  121.8 1.9 %collective-permute-start.4 = (bf16[192,256]{1,0:T(8,128)(2,1)S(1)}, bf16[192,256]{1,0:T(8,128)(2,1)S(1)}, u32[]{:S(2)}, u32[]{:S(2)}) collective-permute-start(bf16[192,256]{1,0:T(8,128)(2,1)S(1)} %get-tuple-element.11), channel_id=1, source_target_pairs={{16,64},{64,16},{17,65},{65,17},{18,66},{66,18},{19,67},{67,19},{2... | collective-permute-start | bytes 294920 | tf_op jit(solution)/shard_map/ppermute | solution.py:268
  123.7 4.4 %collective-permute-start.5 = (bf16[8,4,256]{2,1,0:T(4,128)(2,1)S(1)}, bf16[8,4,256]{2,1,0:T(4,128)(2,1)S(1)}, u32[]{:S(2)}, u32[]{:S(2)}) collective-permute-start(bf16[8,4,256]{2,1,0:T(4,128)(2,1)S(1)} %get-tuple-element.12), channel_id=1, source_target_pairs={{0,32},{32,0},{1,33},{33,1},{2,34},{34,2},{3,35},{35,3},{4,36},{36... | collective-permute-start | bytes 49160 | tf_op jit(solution)/shard_map/ppermute | solution.py:264
  128.1 4.1 %collective-permute-start.6 = (bf16[8,4,256]{2,1,0:T(4,128)(2,1)S(1)}, bf16[8,4,256]{2,1,0:T(4,128)(2,1)S(1)}, u32[]{:S(2)}, u32[]{:S(2)}) collective-permute-start(bf16[8,4,256]{2,1,0:T(4,128)(2,1)S(1)} %get-tuple-element.13), channel_id=1, source_target_pairs={{0,48},{1,49},{2,50},{3,51},{4,52},{5,53},{6,54},{7,55},{8,56},{9,... | collective-permute-start | bytes 49160 | tf_op jit(solution)/shard_map/ppermute | solution.py:265
  132.2 0.0 collective-permute-done.5.keep_y_hbm
  132.2 1.6 %collective-permute-done.6.send_y_hbm = bf16[8,4,256]{2,1,0:T(4,128)(2,1)S(1)} collective-permute-done((bf16[8,4,256]{2,1,0:T(4,128)(2,1)S(1)}, bf16[8,4,256]{2,1,0:T(4,128)(2,1)S(1)}, u32[]{:S(2)}, u32[]{:S(2)}) %collective-permute-start.6) | collective-permute-done | bytes 16416 | tf_op jit(solution)/shard_map/ppermute | solution.py:265
  133.8 0.0 collective-permute-done.3
  133.8 0.0 collective-permute-done.4
  133.8 0.0 collective-permute-done.2
  133.8 0.0 copy-done.1
  133.8 3.7 %stencil.1 = (bf16[16,48,256]{2,1,0:T(8,128)(2,1)}, bf16[16,48,256]{2,1,0:T(8,128)(2,1)}) custom-call(bf16[8,48,256]{2,1,0:T(8,128)(2,1)S(1)} %bitcast.6, bf16[8,48,256]{2,1,0:T(8,128)(2,1)S(1)} %bitcast.7, bf16[4,48,256]{2,1,0:T(8,128)(2,1)S(1)} %bitcast.8, bf16[4,48,256]{2,1,0:T(8,128)(2,1)S(1)} %bitcast.9, ...), custom_call_target="tpu_custom_call" | custom-call | tf_op jit(solution)/shard_map/stencil/pallas_call | solution.py:216
Async XLA Ops:
  7.2 99.0 %all-gather.2.cloned.1.call-start = ((), (), s32[]{:S(2)}) async-start(), calls=%async_computation | async-start | bytes 6684672 | tf_op jit(solution)/shard_map/all_gather | solution.py:245
  8.3 125.5 %copy-start.1 = (f32[4,16,48]{2,1,0:T(8,128)S(1)}, f32[4,16,48]{2,1,0:T(8,128)}, u32[]{:S(2)}) copy-start(f32[4,16,48]{2,1,0:T(8,128)} %levels_hbm.1) | copy-start | bytes 36868
  8.3 7.1 %collective-permute-start.1 = (bf16[8,48,256]{2,1,0:T(8,128)(2,1)S(1)}, bf16[8,48,256]{2,1,0:T(8,128)(2,1)S(1)}, u32[]{:S(2)}, u32[]{:S(2)}) collective-permute-start(bf16[8,48,256]{2,1,0:T(8,128)(2,1)S(1)} %get-tuple-element.15), channel_id=1, source_target_pairs={{0,16},{1,17},{2,18},{3,19},{4,20},{5,21},{6,22},{7,23},{8,24},{9,... | collective-permute-start | bytes 589832 | tf_op jit(solution)/shard_map/ppermute | solution.py:242
  16.2 8.6 %collective-permute-start = (bf16[64,2048]{1,0:T(8,128)(2,1)}, bf16[64,2048]{1,0:T(8,128)(2,1)S(1)}, u32[]{:S(2)}, u32[]{:S(2)}) collective-permute-start(bf16[64,2048]{1,0:T(8,128)(2,1)} %own_ref.1), channel_id=1, source_target_pairs={{0,16},{1,17},{2,18},{3,19},{4,20},{5,21},{6,22},{7,23},{8,24},{9,... | collective-permute-start | bytes 786440 | tf_op jit(solution)/shard_map/ppermute | solution.py:246
  24.8 1.0 copy-start
  112.5 21.2 %collective-permute-start.2 = (bf16[384,256]{1,0:T(8,128)(2,1)S(1)}, bf16[384,256]{1,0:T(8,128)(2,1)S(1)}, u32[]{:S(2)}, u32[]{:S(2)}) collective-permute-start(bf16[384,256]{1,0:T(8,128)(2,1)S(1)} %get-tuple-element.9), channel_id=1, source_target_pairs={{0,16},{1,17},{2,18},{3,19},{4,20},{5,21},{6,22},{7,23},{8,24},{9,... | collective-permute-start | bytes 589832 | tf_op jit(solution)/shard_map/ppermute | solution.py:266
  115.7 18.1 %collective-permute-start.3 = (bf16[192,256]{1,0:T(8,128)(2,1)S(1)}, bf16[192,256]{1,0:T(8,128)(2,1)S(1)}, u32[]{:S(2)}, u32[]{:S(2)}) collective-permute-start(bf16[192,256]{1,0:T(8,128)(2,1)S(1)} %get-tuple-element.10), channel_id=1, source_target_pairs={{16,80},{64,0},{17,81},{65,1},{18,82},{66,2},{19,83},{67,3},{20,84... | collective-permute-start | bytes 294920 | tf_op jit(solution)/shard_map/ppermute | solution.py:267
  121.8 12.0 %collective-permute-start.4 = (bf16[192,256]{1,0:T(8,128)(2,1)S(1)}, bf16[192,256]{1,0:T(8,128)(2,1)S(1)}, u32[]{:S(2)}, u32[]{:S(2)}) collective-permute-start(bf16[192,256]{1,0:T(8,128)(2,1)S(1)} %get-tuple-element.11), channel_id=1, source_target_pairs={{16,64},{64,16},{17,65},{65,17},{18,66},{66,18},{19,67},{67,19},{2... | collective-permute-start | bytes 294920 | tf_op jit(solution)/shard_map/ppermute | solution.py:268
  123.7 8.5 %collective-permute-start.5 = (bf16[8,4,256]{2,1,0:T(4,128)(2,1)S(1)}, bf16[8,4,256]{2,1,0:T(4,128)(2,1)S(1)}, u32[]{:S(2)}, u32[]{:S(2)}) collective-permute-start(bf16[8,4,256]{2,1,0:T(4,128)(2,1)S(1)} %get-tuple-element.12), channel_id=1, source_target_pairs={{0,32},{32,0},{1,33},{33,1},{2,34},{34,2},{3,35},{35,3},{4,36},{36... | collective-permute-start | bytes 49160 | tf_op jit(solution)/shard_map/ppermute | solution.py:264
  128.1 5.7 %collective-permute-start.6 = (bf16[8,4,256]{2,1,0:T(4,128)(2,1)S(1)}, bf16[8,4,256]{2,1,0:T(4,128)(2,1)S(1)}, u32[]{:S(2)}, u32[]{:S(2)}) collective-permute-start(bf16[8,4,256]{2,1,0:T(4,128)(2,1)S(1)} %get-tuple-element.13), channel_id=1, source_target_pairs={{0,48},{1,49},{2,50},{3,51},{4,52},{5,53},{6,54},{7,55},{8,56},{9,... | collective-permute-start | bytes 49160 | tf_op jit(solution)/shard_map/ppermute | solution.py:265
Sparse Core Ops, SparseCore 0:
  16.3 89.7 all-gather.1
